TPU v7x, 256 devices: a whole 4x4x8 slice. The times are simulated.
256 devices in a mesh: lat: 8 (over x, z_hi), lon: 32 (over z_lo, y, core).
Axes of the slice: x: 4, y: 4, z: 8 (z_hi: 2, z_lo: 4; z = z_hi * 4 + z_lo), core: 2. Of those that a mesh axis runs over, the one named last changes fastest.
Arguments:
- fields: bfloat16 [64, 1024, 768], P('lat', 'lon'), may hold values from -60 to 60
- conv_kernel: float32 [3, 3, 768], replicated, may hold values from -1 to 1
- layer_norm_gain: float32 [768], replicated, may hold values from 0.1 to 1.9
- qkv_weight: bfloat16 [768, 2304], replicated, may hold values from -0.21875 to 0.21875
- out_weight: bfloat16 [768, 768], replicated, may hold values from -0.21875 to 0.21875
- score_bias: float32 [24, 64, 64], replicated, may hold values from -4 to 400
- pattern: int32 [8, 32, 256], P('lat', 'lon'), may hold values from 0 to 255, each once within a row
- cotangent: bfloat16 [64, 1024, 768], P('lat', 'lon'), may hold values from -6 to 6
Outputs:
- block_out: bfloat16 [64, 1024, 768], P('lat', 'lon')
- grad_fields: bfloat16 [64, 1024, 768], P('lat', 'lon')
- grad_project: float32 [768, 768], P('lat', 'lon')
- grad_kernel: float32 [3, 3, 768], replicated
- gain_gradient: float32 [768], replicated
Inputs may be any that keep to these rules, and one draw needn't show every extreme that they name: pattern[a, b, :] lists each of the 256 cells of block (a, b) once.
All inputs are finite; a program needn't handle non-finite values.
Results may differ from a plain program's by a relative error of at most 0.028.
Values may be sent and summed in bfloat16 or wider, within the bound.
A program may use at most 128 MiB of HBM per device.

v0:
```python
import math
import jax
import jax.numpy as jnp
from jax import lax
from jax.sharding import PartitionSpec as P

HEADS = 24
HEAD_DIM = 32
GROUP = 64
epsilon = 1e-05


def extended(array, sides, width, wrap):
    for axis, dim in sides:
        peers, length = (lax.axis_size(axis), array.shape[dim])
        up = [(i, (i + 1) % peers) for i in range(peers if wrap else peers - 1)]
        down = [(j, i) for i, j in up]
        last = lax.slice_in_dim(array, length - width, length, axis=dim)
        first = lax.slice_in_dim(array, 0, width, axis=dim)
        before = lax.ppermute(last, axis, up)
        after = lax.ppermute(first, axis, down)
        array = jnp.concatenate([before, array, after], axis=dim)
    return array


def widened(field):
    beside_all = extended(field, (("lon", 1),), 1, True)
    return extended(beside_all, (("lat", 0),), 1, False)


def apply_taps(padded, conv_kernel, lat_rows, lon_cols):
    summed = jnp.zeros((lat_rows, lon_cols, padded.shape[2]), jnp.float32)
    for lat_tap in range(3):
        for lon_tap in range(3):
            summed = (
                summed
                + conv_kernel[lat_tap, lon_tap]
                * padded[lat_tap : lat_tap + lat_rows, lon_tap : lon_tap + lon_cols]
            )
    return summed


def to_owner(packed):
    arrived = lax.all_to_all(
        lax.all_to_all(packed, "lat", split_axis=0, concat_axis=3, tiled=True),
        "lon",
        split_axis=1,
        concat_axis=4,
        tiled=True,
    )
    return arrived.reshape(-1, arrived.shape[-1])


def to_grid(packed):
    arrived = lax.all_to_all(
        lax.all_to_all(packed, "lat", split_axis=3, concat_axis=0, tiled=True),
        "lon",
        split_axis=4,
        concat_axis=1,
        tiled=True,
    )
    return arrived.reshape(-1, arrived.shape[-1])


def attention_probs(queries, key_rows, score_bias):
    scores = jnp.einsum("gihd,gjhd->ghij", queries, key_rows, preferred_element_type=jnp.float32)
    scores = scores * queries.shape[-1] ** (-0.5) + score_bias[None]
    peak = jnp.max(scores, axis=-1, keepdims=True)
    lifted = jnp.exp(scores - peak)
    return lifted / jnp.sum(lifted, axis=-1, keepdims=True)


def body(
    fields, conv_kernel, layer_norm_gain, qkv_weight, out_weight, score_bias, pattern, cotangent
):
    lat_rows, lon_cols, feature_count = fields.shape
    cell_count = lat_rows * lon_cols
    lat_count = lax.axis_size("lat")
    lon_count = lax.axis_size("lon")
    slot_count = cell_count // (lat_count * lon_count)
    scale_everywhere = 1.0 / math.sqrt(cell_count * lat_count * lon_count)
    head_scale = HEAD_DIM ** (-0.5)
    group_count = cell_count // GROUP
    slot_order = pattern.reshape(cell_count)
    inverse = (
        jnp.zeros((cell_count,), jnp.int32)
        .at[slot_order]
        .set(jnp.arange(cell_count, dtype=jnp.int32))
    )

    def outward(field):
        picked = jnp.take(field.reshape(cell_count, feature_count), slot_order, axis=0)
        return picked.reshape(lat_count, lon_count, slot_count, 1, 1, feature_count)

    def inward(grouped):
        return grouped.reshape(1, 1, slot_count, lat_count, lon_count, grouped.shape[-1])

    def homeward(flat):
        return jnp.take(flat, inverse, axis=0).reshape(lat_rows, lon_cols, feature_count)

    padded_fields = widened(fields)
    state_h = (
        fields.astype(jnp.float32) + apply_taps(padded_fields, conv_kernel, lat_rows, lon_cols)
    ).astype(jnp.bfloat16)
    state_f = state_h.astype(jnp.float32)
    mean_h = jnp.mean(state_f, axis=-1, keepdims=True)
    mean_removed = state_f - mean_h
    var_h = jnp.mean(mean_removed * mean_removed, axis=-1, keepdims=True)
    inverse_deviation = lax.rsqrt(var_h + epsilon)
    standardized_input = mean_removed * inverse_deviation
    normalized_fields = (standardized_input * layer_norm_gain).astype(jnp.bfloat16)
    normed_g = to_owner(outward(normalized_fields))
    cot_g = to_owner(outward(cotangent))
    qkv_rows = jnp.dot(normed_g, qkv_weight, preferred_element_type=jnp.float32).astype(
        jnp.bfloat16
    )
    split_rows = qkv_rows.reshape(group_count, GROUP, 3, HEADS, HEAD_DIM)
    queries = split_rows[:, :, 0]
    key_rows = split_rows[:, :, 1]
    value_rows = split_rows[:, :, 2]
    probs = attention_probs(queries, key_rows, score_bias)
    probs_low = probs.astype(jnp.bfloat16)
    attended = jnp.einsum(
        "ghij,gjhd->gihd", probs_low, value_rows, preferred_element_type=jnp.float32
    )
    attended = attended.astype(jnp.bfloat16).reshape(cell_count, feature_count)
    mixed = jnp.dot(attended, out_weight, preferred_element_type=jnp.float32).astype(jnp.bfloat16)
    mixed_flat = to_grid(inward(mixed))
    rows_summed = lax.psum_scatter(
        lax.dot_general(
            attended, cot_g, (((0,), (0,)), ((), ())), preferred_element_type=jnp.float32
        ).astype(jnp.bfloat16),
        "lat",
        scatter_dimension=0,
        tiled=True,
    )
    grad_project = (
        lax.psum_scatter(rows_summed, "lon", scatter_dimension=1, tiled=True).astype(jnp.float32)
        * scale_everywhere
    )
    grad_att = lax.dot_general(
        cot_g, out_weight, (((1,), (1,)), ((), ())), preferred_element_type=jnp.float32
    ).astype(jnp.bfloat16)
    grad_heads = grad_att.reshape(group_count, GROUP, HEADS, HEAD_DIM)
    held_query, held_key = (queries, key_rows)
    grad_probs = jnp.einsum(
        "gihd,gjhd->ghij", grad_heads, value_rows, preferred_element_type=jnp.float32
    )
    grad_scores = probs * (grad_probs - jnp.sum(probs * grad_probs, axis=-1, keepdims=True))
    grad_scores = grad_scores.astype(jnp.bfloat16)
    grad_query = (
        jnp.einsum("ghij,gjhd->gihd", grad_scores, held_key, preferred_element_type=jnp.float32)
        * head_scale
    )
    grad_key = (
        jnp.einsum("ghij,gihd->gjhd", grad_scores, held_query, preferred_element_type=jnp.float32)
        * head_scale
    )
    grad_value = jnp.einsum(
        "ghij,gihd->gjhd", probs_low, grad_heads, preferred_element_type=jnp.float32
    )
    grad_qkv = jnp.stack([grad_query, grad_key, grad_value], axis=2).astype(jnp.bfloat16)
    grad_qkv = grad_qkv.reshape(cell_count, 3 * feature_count)
    grad_grouped = lax.dot_general(
        grad_qkv, qkv_weight, (((1,), (1,)), ((), ())), preferred_element_type=jnp.float32
    ).astype(jnp.bfloat16)
    grad_flat = to_grid(inward(grad_grouped))
    block_out = (state_f + homeward(mixed_flat).astype(jnp.float32)).astype(jnp.bfloat16)
    normalized_gradient = homeward(grad_flat).astype(jnp.float32)
    gain_on_device = jnp.sum(normalized_gradient * standardized_input, axis=(0, 1))
    gain_scaled = normalized_gradient * layer_norm_gain
    layer_norm_gradient = inverse_deviation * (
        gain_scaled
        - jnp.mean(gain_scaled, axis=-1, keepdims=True)
        - standardized_input * jnp.mean(gain_scaled * standardized_input, axis=-1, keepdims=True)
    )
    grad_h = (cotangent.astype(jnp.float32) + layer_norm_gradient).astype(jnp.bfloat16)
    grad_hf = grad_h.astype(jnp.float32)
    padded_grad = widened(grad_h)
    grad_fields = (
        grad_hf + apply_taps(padded_grad, conv_kernel[::-1, ::-1], lat_rows, lon_cols)
    ).astype(jnp.bfloat16)
    kernel_terms = []
    for lat_tap in range(3):
        for lon_tap in range(3):
            kernel_terms.append(
                jnp.sum(
                    padded_fields[lat_tap : lat_tap + lat_rows, lon_tap : lon_tap + lon_cols]
                    * grad_hf,
                    axis=(0, 1),
                )
            )
    kernel_local = jnp.stack(kernel_terms).reshape(3, 3, feature_count)
    gain_total, kernel_total = lax.psum((gain_on_device, kernel_local), ("lat", "lon"))
    return (
        block_out,
        grad_fields,
        grad_project,
        kernel_total * scale_everywhere,
        gain_total * scale_everywhere,
    )


def solution(mesh):
    placed = (
        P("lat", "lon", None),
        P(),
        P(),
        P(),
        P(),
        P(),
        P("lat", "lon", None),
        P("lat", "lon", None),
    )
    return jax.shard_map(
        body,
        mesh=mesh,
        in_specs=placed,
        out_specs=(P("lat", "lon", None), P("lat", "lon", None), P("lat", "lon"), P(), P()),
        check_vma=False,
    )
```

profile of v0, /device:TPU:1, one launch (start us, length us, event | category | flops | bytes accessed | tf_op | source)
XLA Modules:
  0.0 629.2 jit_solution(4152701214273472165)
XLA Ops:
  17.3 8.8 %collective-permute-start.2 = (bf16[1,34,768]{2,1,0:T(8,128)(2,1)}, bf16[1,34,768]{2,1,0:T(8,128)(2,1)}, u32[]{:S(2)}, u32[]{:S(2)}) collective-permute-start(bf16[1,34,768]{2,1,0:T(8,128)(2,1)} %get-tuple-element.66), channel_id=1, source_target_pairs={{0,32},{32,64},{64,96},{96,128},{128,160},{160,192},{192,224},{1,3... | collective-permute-start | bytes 156680 | tf_op jit(solution)/shard_map/ppermute | solution.py:20
  30.7 4.7 collective-permute-done.3
  45.4 15.7 %all_to_all.108 = bf16[8,32,1,1,1,768]{5,1,4,3,2,0:T(8,128)(2,1)} all-to-all(bf16[8,32,1,1,1,768]{5,1,4,3,2,0:T(8,128)(2,1)S(1)} %bitcast.110), channel_id=1, replica_groups=mesh['lat'=8,'lon'=32] {'lat'}, dimensions={0} | all-to-all | bytes 786432 | tf_op jit(solution)/shard_map/all_to_all | solution.py:45
  61.1 4.1 all-to-all-start
  67.2 8.8 %all-to-all-done = bf16[8,32,1,1,1,768]{5,1,4,3,2,0:T(8,128)(2,1)} async-done(((bf16[8,32,1,1,1,768]{5,1,4,3,2,0:T(8,128)(2,1)}), bf16[8,32,1,1,1,768]{5,1,4,3,2,0:T(8,128)(2,1)}, u32[]{:S(2)}, u32[]{:S(2)}) %all-to-all-start) | async-done | bytes 393248 | tf_op jit(solution)/shard_map/all_to_all | solution.py:45
  75.9 17.9 %all-to-all-start.5 = ((bf16[1,32,1,8,1,768]{5,3,4,2,0,1:T(8,128)(2,1)}), bf16[1,32,1,8,1,768]{5,3,4,2,0,1:T(8,128)(2,1)}, u32[]{:S(2)}, u32[]{:S(2)}) async-start(bf16[1,32,1,8,1,768]{5,3,4,2,0,1:T(8,128)(2,1)} %copy.78), calls=%async_computation.5 | async-start | bytes 786432 | tf_op jit(solution)/shard_map/all_to_all | solution.py:44
  95.8 11.9 %all-to-all-done.5 = bf16[1,32,1,8,1,768]{5,3,4,2,0,1:T(8,128)(2,1)} async-done(((bf16[1,32,1,8,1,768]{5,3,4,2,0,1:T(8,128)(2,1)}), bf16[1,32,1,8,1,768]{5,3,4,2,0,1:T(8,128)(2,1)}, u32[]{:S(2)}, u32[]{:S(2)}) %all-to-all-start.5) | async-done | bytes 393248 | tf_op jit(solution)/shard_map/all_to_all | solution.py:44
  107.6 4.8 all-to-all-start.1
  131.8 4.6 reshape.150
  155.4 4.3 all-to-all-start.2
  159.6 3.9 multiply_convert_fusion
  166.4 4.5 copy.86
  170.8 4.5 convert_element_type.159
  178.5 9.0 %all-to-all-start.6 = ((bf16[1,1,1,8,32,768]{5,4,2,1,0,3:T(8,128)(2,1)}), bf16[1,1,1,8,32,768]{5,4,2,1,0,3:T(8,128)(2,1)}, u32[]{:S(2)}, u32[]{:S(2)}) async-start(bf16[1,1,1,8,32,768]{5,4,2,1,0,3:T(8,128)(2,1)} %bitcast.112), calls=%async_computation.6 | async-start | bytes 786432 | tf_op jit(solution)/shard_map/all_to_all | solution.py:56
  189.5 10.5 %all-to-all-done.6 = bf16[1,1,1,8,32,768]{5,4,2,1,0,3:T(8,128)(2,1)} async-done(((bf16[1,1,1,8,32,768]{5,4,2,1,0,3:T(8,128)(2,1)}), bf16[1,1,1,8,32,768]{5,4,2,1,0,3:T(8,128)(2,1)}, u32[]{:S(2)}, u32[]{:S(2)}) %all-to-all-start.6) | async-done | bytes 393248 | tf_op jit(solution)/shard_map/all_to_all | solution.py:56
  199.9 9.4 %all-to-all-start.3 = ((bf16[8,1,1,1,32,768]{5,0,3,2,1,4:T(8,128)(2,1)}), bf16[8,1,1,1,32,768]{5,0,3,2,1,4:T(8,128)(2,1)}, u32[]{:S(2)}, u32[]{:S(2)}) async-start(bf16[8,1,1,1,32,768]{5,0,3,2,1,4:T(8,128)(2,1)} %copy.75), calls=%async_computation.3 | async-start | bytes 786432 | tf_op jit(solution)/shard_map/all_to_all | solution.py:55
  217.1 6.0 all-to-all-done.3
  223.1 4.4 all-to-all-start.7
  234.8 3.4 gather_fusion.1
  267.4 77.1 %all-reduce.1 = (f32[3,3,768]{2,1,0:T(4,128)}, f32[768]{0:T(1024)}) all-reduce(f32[3,3,768]{2,1,0:T(4,128)} %reshape.161, f32[768]{0:T(1024)} %get-tuple-element.35), channel_id=1, replica_groups=mesh['lat'=8,'lon'=32] {'lat','lon'}, use_global_device_ids=true, to_apply=%region_19.21 | all-reduce | flops 7680 | bytes 61440 | tf_op jit(solution)/shard_map/psum | solution.py:194
  346.8 3.8 collective-permute-start.6
  353.1 6.3 collective-permute-done.7
  362.1 4.3 fusion.36
  366.4 252.8 %all-reduce.4.cloned.1.call-done = bf16[96,768]{1,0:T(8,128)(2,1)} async-done(((bf16[96,768]{1,0:T(8,128)(2,1)}), bf16[96,768]{1,0:T(8,128)(2,1)}) %all-reduce.4.cloned.1.call-update) | async-done | bytes 147472
  (180 shorter events, 128.6 us)
Async XLA Ops:
  7.2 120.1 %copy-start = (bf16[768,2304]{1,0:T(8,128)(2,1)S(1)}, bf16[768,2304]{1,0:T(8,128)(2,1)}, u32[]{:S(2)}) copy-start(bf16[768,2304]{1,0:T(8,128)(2,1)} %param.13) | copy-start | bytes 10616836
  8.3 6.9 %collective-permute-start = (bf16[8,1,768]{2,1,0:T(2,128)(2,1)S(1)}, bf16[8,1,768]{2,1,0:T(2,128)(2,1)S(1)}, u32[]{:S(2)}, u32[]{:S(2)}) collective-permute-start(bf16[8,1,768]{2,1,0:T(2,128)(2,1)S(1)} %get-tuple-element.71), channel_id=1, source_target_pairs={{0,1},{1,2},{2,3},{3,4},{4,5},{5,6},{6,7},{7,8},{8,9},{9,10},{10,1... | collective-permute-start | bytes 36872 | tf_op jit(solution)/shard_map/ppermute | solution.py:20
  11.1 4.1 collective-permute-start.1
  15.2 23.2 %copy-start.28 = (f32[768]{0:T(1024)}, f32[768]{0:T(1024)S(1)}, u32[]{:S(2)}) copy-start(f32[768]{0:T(1024)S(1)} %get-tuple-element.44) | copy-start | bytes 9220
  15.2 23.2 %copy-start.30 = (f32[768]{0:T(1024)}, f32[768]{0:T(1024)S(1)}, u32[]{:S(2)}) copy-start(f32[768]{0:T(1024)S(1)} %get-tuple-element.45) | copy-start | bytes 9220
  17.3 13.4 %collective-permute-start.2 = (bf16[1,34,768]{2,1,0:T(8,128)(2,1)}, bf16[1,34,768]{2,1,0:T(8,128)(2,1)}, u32[]{:S(2)}, u32[]{:S(2)}) collective-permute-start(bf16[1,34,768]{2,1,0:T(8,128)(2,1)} %get-tuple-element.66), channel_id=1, source_target_pairs={{0,32},{32,64},{64,96},{96,128},{128,160},{160,192},{192,224},{1,3... | collective-permute-start | bytes 156680 | tf_op jit(solution)/shard_map/ppermute | solution.py:20
  26.1 9.3 %collective-permute-start.3 = (bf16[1,34,768]{2,1,0:T(8,128)(2,1)}, bf16[1,34,768]{2,1,0:T(8,128)(2,1)}, u32[]{:S(2)}, u32[]{:S(2)}) collective-permute-start(bf16[1,34,768]{2,1,0:T(8,128)(2,1)} %get-tuple-element.67), channel_id=1, source_target_pairs={{32,0},{64,32},{96,64},{128,96},{160,128},{192,160},{224,192},{33,... | collective-permute-start | bytes 156680 | tf_op jit(solution)/shard_map/ppermute | solution.py:21
  30.6 6.5 %copy-start.32 = (f32[768]{0:T(1024)S(1)}, f32[768]{0:T(1024)}, u32[]{:S(2)}) copy-start(f32[768]{0:T(1024)} %get-tuple-element.46) | copy-start | bytes 9220
  61.1 14.9 %all-to-all-start = ((bf16[8,32,1,1,1,768]{5,1,4,3,2,0:T(8,128)(2,1)}), bf16[8,32,1,1,1,768]{5,1,4,3,2,0:T(8,128)(2,1)}, u32[]{:S(2)}, u32[]{:S(2)}) async-start(bf16[8,32,1,1,1,768]{5,1,4,3,2,0:T(8,128)(2,1)} %bitcast.109), calls=%async_computation | async-start | bytes 786432 | tf_op jit(solution)/shard_map/all_to_all | solution.py:45
  75.9 31.7 %all-to-all-start.5 = ((bf16[1,32,1,8,1,768]{5,3,4,2,0,1:T(8,128)(2,1)}), bf16[1,32,1,8,1,768]{5,3,4,2,0,1:T(8,128)(2,1)}, u32[]{:S(2)}, u32[]{:S(2)}) async-start(bf16[1,32,1,8,1,768]{5,3,4,2,0,1:T(8,128)(2,1)} %copy.78), calls=%async_computation.5 | async-start | bytes 786432 | tf_op jit(solution)/shard_map/all_to_all | solution.py:44
  107.6 18.6 %all-to-all-start.1 = ((bf16[1,32,1,8,1,768]{5,3,4,2,0,1:T(8,128)(2,1)}), bf16[1,32,1,8,1,768]{5,3,4,2,0,1:T(8,128)(2,1)}, u32[]{:S(2)}, u32[]{:S(2)}) async-start(bf16[1,32,1,8,1,768]{5,3,4,2,0,1:T(8,128)(2,1)} %copy.65), calls=%async_computation.1 | async-start | bytes 786432 | tf_op jit(solution)/shard_map/all_to_all | solution.py:44
  155.4 23.1 %all-to-all-start.2 = ((bf16[1,1,1,8,32,768]{5,4,2,1,0,3:T(8,128)(2,1)}), bf16[1,1,1,8,32,768]{5,4,2,1,0,3:T(8,128)(2,1)}, u32[]{:S(2)}, u32[]{:S(2)}) async-start(bf16[1,1,1,8,32,768]{5,4,2,1,0,3:T(8,128)(2,1)} %bitcast.111), calls=%async_computation.2 | async-start | bytes 786432 | tf_op jit(solution)/shard_map/all_to_all | solution.py:56
  178.5 21.4 %all-to-all-start.6 = ((bf16[1,1,1,8,32,768]{5,4,2,1,0,3:T(8,128)(2,1)}), bf16[1,1,1,8,32,768]{5,4,2,1,0,3:T(8,128)(2,1)}, u32[]{:S(2)}, u32[]{:S(2)}) async-start(bf16[1,1,1,8,32,768]{5,4,2,1,0,3:T(8,128)(2,1)} %bitcast.112), calls=%async_computation.6 | async-start | bytes 786432 | tf_op jit(solution)/shard_map/all_to_all | solution.py:56
  199.9 23.2 %all-to-all-start.3 = ((bf16[8,1,1,1,32,768]{5,0,3,2,1,4:T(8,128)(2,1)}), bf16[8,1,1,1,32,768]{5,0,3,2,1,4:T(8,128)(2,1)}, u32[]{:S(2)}, u32[]{:S(2)}) async-start(bf16[8,1,1,1,32,768]{5,0,3,2,1,4:T(8,128)(2,1)} %copy.75), calls=%async_computation.3 | async-start | bytes 786432 | tf_op jit(solution)/shard_map/all_to_all | solution.py:55
  223.1 18.1 %all-to-all-start.7 = ((bf16[8,1,1,1,32,768]{5,0,3,2,1,4:T(8,128)(2,1)}), bf16[8,1,1,1,32,768]{5,0,3,2,1,4:T(8,128)(2,1)}, u32[]{:S(2)}, u32[]{:S(2)}) async-start(bf16[8,1,1,1,32,768]{5,0,3,2,1,4:T(8,128)(2,1)} %copy.88), calls=%async_computation.7 | async-start | bytes 786432 | tf_op jit(solution)/shard_map/all_to_all | solution.py:55
  227.5 134.6 %reduce-scatter.3.cloned.1.call-start = ((), (), s32[]{:S(2)}) async-start(), calls=%async_computation.9 | async-start | bytes 1327104 | tf_op jit(solution)/shard_map/reduce_scatter | solution.py:129
  230.2 389.0 %all-reduce.4.cloned.1.call-start = ((), (), s32[]{:S(2)}) async-start(), calls=%async_computation.10 | async-start | bytes 294912
  255.9 106.2 %copy-start.29 = (f32[768]{0:T(1024)S(1)}, f32[768]{0:T(1024)}, u32[]{:S(2)}) copy-start(f32[768]{0:T(1024)} %copy-done.28) | copy-start | bytes 9220
  255.9 106.2 %copy-start.31 = (f32[768]{0:T(1024)S(1)}, f32[768]{0:T(1024)}, u32[]{:S(2)}) copy-start(f32[768]{0:T(1024)} %copy-done.30) | copy-start | bytes 9220
  255.9 106.2 %copy-start.33 = (f32[768]{0:T(1024)S(1)}, f32[768]{0:T(1024)}, u32[]{:S(2)}) copy-start(f32[768]{0:T(1024)} %get-tuple-element.46) | copy-start | bytes 9220
  266.9 79.0 %collective-permute-start.4 = (bf16[8,1,768]{2,1,0:T(2,128)(2,1)}, bf16[8,1,768]{2,1,0:T(2,128)(2,1)}, u32[]{:S(2)}, u32[]{:S(2)}) collective-permute-start(bf16[8,1,768]{2,1,0:T(2,128)(2,1)} %get-tuple-element.68), channel_id=1, source_target_pairs={{0,1},{1,2},{2,3},{3,4},{4,5},{5,6},{6,7},{7,8},{8,9},{9,10},{10,1... | collective-permute-start | bytes 36872 | tf_op jit(solution)/shard_map/ppermute | solution.py:20
  266.9 79.0 %collective-permute-start.5 = (bf16[8,1,768]{2,1,0:T(2,128)(2,1)}, bf16[8,1,768]{2,1,0:T(2,128)(2,1)}, u32[]{:S(2)}, u32[]{:S(2)}) collective-permute-start(bf16[8,1,768]{2,1,0:T(2,128)(2,1)} %get-tuple-element.69), channel_id=1, source_target_pairs={{1,0},{2,1},{3,2},{4,3},{5,4},{6,5},{7,6},{8,7},{9,8},{10,9},{11,1... | collective-permute-start | bytes 36872 | tf_op jit(solution)/shard_map/ppermute | solution.py:21
  346.8 6.4 %collective-permute-start.6 = (bf16[1,34,768]{2,1,0:T(8,128)(2,1)S(1)}, bf16[1,34,768]{2,1,0:T(8,128)(2,1)S(1)}, u32[]{:S(2)}, u32[]{:S(2)}) collective-permute-start(bf16[1,34,768]{2,1,0:T(8,128)(2,1)S(1)} %get-tuple-element.62), channel_id=1, source_target_pairs={{0,32},{32,64},{64,96},{96,128},{128,160},{160,192},{192,224},{1,3... | collective-permute-start | bytes 156680 | tf_op jit(solution)/shard_map/ppermute | solution.py:20
  350.5 8.9 %collective-permute-start.7 = (bf16[1,34,768]{2,1,0:T(8,128)(2,1)S(1)}, bf16[1,34,768]{2,1,0:T(8,128)(2,1)S(1)}, u32[]{:S(2)}, u32[]{:S(2)}) collective-permute-start(bf16[1,34,768]{2,1,0:T(8,128)(2,1)S(1)} %get-tuple-element.63), channel_id=1, source_target_pairs={{32,0},{64,32},{96,64},{128,96},{160,128},{192,160},{224,192},{33,... | collective-permute-start | bytes 156680 | tf_op jit(solution)/shard_map/ppermute | solution.py:21
  (35 other events, 96.6 us)
Sparse Core Ops, SparseCore 0:
  232.3 83.6 reduce-scatter.2
  362.2 256.9 all-reduce.3
where the time goes:
time: 638 us; the launch traced here: 629 us
  waiting for transfers between devices  307 us (48%)
  blocking collectives  92.7 us (15%)
  local copies, waits for them, and re-layouts  80.9 us (13%)
  starting transfers between devices  73.1 us (11%)
  other arithmetic  39.4 us (6%)
  matrix products  20.8 us (3%)
  between operations  15.6 us (2%)
    unnamed x3, waiting for transfers between devices  253 us
    psum x1, blocking collectives, body(): lax.psum((gain_on_device, kernel_local), ('lat', 'lon'))  77.1 us
    all_to_all x2, starting transfers between devices, to_owner(): lax.all_to_all(lax.all_to_all(packed, 'lat', split_axis=0, concat_axis=3,...  22.7 us
    all_to_all x1, blocking collectives, to_owner(): lax.all_to_all(packed, 'lat', split_axis=0, concat_axis=3, tiled=True)  15.7 us
    ppermute x4, starting transfers between devices, extended(): before = lax.ppermute(last, axis, up)  15.3 us
    all_to_all x2, waiting for transfers between devices, to_owner(): lax.all_to_all(lax.all_to_all(packed, 'lat', split_axis=0, concat_axis=3,...  14.5 us
    all_to_all x2, starting transfers between devices, to_grid(): lax.all_to_all(lax.all_to_all(packed, 'lat', split_axis=3, concat_axis=0,...  13.7 us
    all_to_all x2, starting transfers between devices, to_grid(): lax.all_to_all(packed, 'lat', split_axis=3, concat_axis=0, tiled=True)  13.3 us
  transfers between devices with their start and end apart: 17, of which 9 were waited for; matrix products, arithmetic and copies ran while one was open for 15% of the time, Pallas kernels for 0%

commit v1 on v0

--- a/solution.py
+++ b/solution.py
@@ -8,6 +8,11 @@
 HEAD_DIM = 32
 GROUP = 64
 epsilon = 1e-05
+
+
+def by_each_axis(x, leading, second):
+    inner = lax.psum(x, leading)
+    return lax.psum(inner, second)
 
 
 def extended(array, sides, width, wrap):
@@ -191,7 +196,7 @@
                 )
             )
     kernel_local = jnp.stack(kernel_terms).reshape(3, 3, feature_count)
-    gain_total, kernel_total = lax.psum((gain_on_device, kernel_local), ("lat", "lon"))
+    gain_total, kernel_total = by_each_axis((gain_on_device, kernel_local), "lon", "lat")
     return (
         block_out,
         grad_fields,

time: 638 us -> 744 us (1.17)
  blocking collectives: 92.7 us -> 191 us
    psum x1 -> x2, blocking collectives: 77.1 us -> 175 us  [the longest x1 133 us: by_each_axis(): inner = lax.psum(x, leading)]
  transfers between devices with their start and end apart: 17 -> 17, of which waited for: 9 -> 9; matrix products, arithmetic and copies ran while one was open for 15% -> 13% of each run, Pallas kernels for 0% -> 0%
where the time goes in v1:
time: 744 us; the launch traced here: 735 us
  waiting for transfers between devices  314 us (42%)
  blocking collectives  191 us (26%)
  local copies, waits for them, and re-layouts  80.9 us (11%)
  starting transfers between devices  74.5 us (10%)
  other arithmetic  39.4 us (5%)
  matrix products  20.8 us (3%)
  between operations  15.6 us (2%)
    unnamed x3, waiting for transfers between devices  260 us
    psum x1, blocking collectives, by_each_axis(): inner = lax.psum(x, leading)  133 us
    psum x1, blocking collectives, by_each_axis(): return lax.psum(inner, second)  42.2 us
    all_to_all x2, starting transfers between devices, to_owner(): lax.all_to_all(lax.all_to_all(packed, 'lat', split_axis=0, concat_axis=3,...  22.7 us
    ppermute x4, starting transfers between devices, extended(): before = lax.ppermute(last, axis, up)  16.7 us
    all_to_all x1, blocking collectives, to_owner(): lax.all_to_all(packed, 'lat', split_axis=0, concat_axis=3, tiled=True)  15.7 us
  transfers between devices with their start and end apart: 17, of which 9 were waited for; matrix products, arithmetic and copies ran while one was open for 13% of the time, Pallas kernels for 0%

profile of v1, /device:TPU:1, one launch (start us, length us, event | category | flops | bytes accessed | tf_op | source)
XLA Modules:
  0.0 735.4 jit_solution(12968204848414138158)
XLA Ops:
  17.3 8.8 %collective-permute-start.2 = (bf16[1,34,768]{2,1,0:T(8,128)(2,1)}, bf16[1,34,768]{2,1,0:T(8,128)(2,1)}, u32[]{:S(2)}, u32[]{:S(2)}) collective-permute-start(bf16[1,34,768]{2,1,0:T(8,128)(2,1)} %get-tuple-element.68), channel_id=1, source_target_pairs={{0,32},{32,64},{64,96},{96,128},{128,160},{160,192},{192,224},{1,3... | collective-permute-start | bytes 156680 | tf_op jit(solution)/shard_map/ppermute | solution.py:25
  30.7 4.7 collective-permute-done.3
  45.4 15.7 %all_to_all.108 = bf16[8,32,1,1,1,768]{5,1,4,3,2,0:T(8,128)(2,1)} all-to-all(bf16[8,32,1,1,1,768]{5,1,4,3,2,0:T(8,128)(2,1)S(1)} %bitcast.110), channel_id=1, replica_groups=mesh['lat'=8,'lon'=32] {'lat'}, dimensions={0} | all-to-all | bytes 786432 | tf_op jit(solution)/shard_map/all_to_all | solution.py:50
  61.1 4.1 all-to-all-start
  67.2 8.8 %all-to-all-done = bf16[8,32,1,1,1,768]{5,1,4,3,2,0:T(8,128)(2,1)} async-done(((bf16[8,32,1,1,1,768]{5,1,4,3,2,0:T(8,128)(2,1)}), bf16[8,32,1,1,1,768]{5,1,4,3,2,0:T(8,128)(2,1)}, u32[]{:S(2)}, u32[]{:S(2)}) %all-to-all-start) | async-done | bytes 393248 | tf_op jit(solution)/shard_map/all_to_all | solution.py:50
  75.9 17.9 %all-to-all-start.5 = ((bf16[1,32,1,8,1,768]{5,3,4,2,0,1:T(8,128)(2,1)}), bf16[1,32,1,8,1,768]{5,3,4,2,0,1:T(8,128)(2,1)}, u32[]{:S(2)}, u32[]{:S(2)}) async-start(bf16[1,32,1,8,1,768]{5,3,4,2,0,1:T(8,128)(2,1)} %copy.78), calls=%async_computation.5 | async-start | bytes 786432 | tf_op jit(solution)/shard_map/all_to_all | solution.py:49
  95.8 11.9 %all-to-all-done.5 = bf16[1,32,1,8,1,768]{5,3,4,2,0,1:T(8,128)(2,1)} async-done(((bf16[1,32,1,8,1,768]{5,3,4,2,0,1:T(8,128)(2,1)}), bf16[1,32,1,8,1,768]{5,3,4,2,0,1:T(8,128)(2,1)}, u32[]{:S(2)}, u32[]{:S(2)}) %all-to-all-start.5) | async-done | bytes 393248 | tf_op jit(solution)/shard_map/all_to_all | solution.py:49
  107.6 4.8 all-to-all-start.1
  131.8 4.6 reshape.150
  155.4 4.3 all-to-all-start.2
  159.6 3.9 multiply_convert_fusion
  166.4 4.5 copy.86
  170.8 4.5 convert_element_type.159
  178.5 9.0 %all-to-all-start.6 = ((bf16[1,1,1,8,32,768]{5,4,2,1,0,3:T(8,128)(2,1)}), bf16[1,1,1,8,32,768]{5,4,2,1,0,3:T(8,128)(2,1)}, u32[]{:S(2)}, u32[]{:S(2)}) async-start(bf16[1,1,1,8,32,768]{5,4,2,1,0,3:T(8,128)(2,1)} %bitcast.112), calls=%async_computation.6 | async-start | bytes 786432 | tf_op jit(solution)/shard_map/all_to_all | solution.py:61
  189.5 10.5 %all-to-all-done.6 = bf16[1,1,1,8,32,768]{5,4,2,1,0,3:T(8,128)(2,1)} async-done(((bf16[1,1,1,8,32,768]{5,4,2,1,0,3:T(8,128)(2,1)}), bf16[1,1,1,8,32,768]{5,4,2,1,0,3:T(8,128)(2,1)}, u32[]{:S(2)}, u32[]{:S(2)}) %all-to-all-start.6) | async-done | bytes 393248 | tf_op jit(solution)/shard_map/all_to_all | solution.py:61
  199.9 9.4 %all-to-all-start.3 = ((bf16[8,1,1,1,32,768]{5,0,3,2,1,4:T(8,128)(2,1)}), bf16[8,1,1,1,32,768]{5,0,3,2,1,4:T(8,128)(2,1)}, u32[]{:S(2)}, u32[]{:S(2)}) async-start(bf16[8,1,1,1,32,768]{5,0,3,2,1,4:T(8,128)(2,1)} %copy.75), calls=%async_computation.3 | async-start | bytes 786432 | tf_op jit(solution)/shard_map/all_to_all | solution.py:60
  217.1 6.0 all-to-all-done.3
  223.1 4.4 all-to-all-start.7
  267.4 132.6 %all-reduce.1 = (f32[3,3,768]{2,1,0:T(4,128)}, f32[768]{0:T(1024)}) all-reduce(f32[3,3,768]{2,1,0:T(4,128)} %reshape.161, f32[768]{0:T(1024)} %get-tuple-element.35), channel_id=1, replica_groups=mesh['lat'=8,'lon'=32] {'lon'}, use_global_device_ids=true, to_apply=%region_19.21 | all-reduce | flops 7680 | bytes 61440 | tf_op jit(solution)/shard_map/psum | solution.py:14
  400.1 42.2 %all-reduce.2 = (f32[3,3,768]{2,1,0:T(4,128)}, f32[768]{0:T(1024)}) all-reduce(f32[3,3,768]{2,1,0:T(4,128)} %get-tuple-element.52, f32[768]{0:T(1024)} %get-tuple-element.53), channel_id=1, replica_groups=mesh['lat'=8,'lon'=32] {'lat'}, use_global_device_ids=true, to_apply=%region_20.22 | all-reduce | flops 7680 | bytes 61440 | tf_op jit(solution)/shard_map/psum | solution.py:15
  444.6 5.1 collective-permute-start.6
  452.3 6.3 collective-permute-done.7
  461.3 4.3 fusion.36
  465.6 259.8 %all-reduce.5.cloned.1.call-done = bf16[96,768]{1,0:T(8,128)(2,1)} async-done(((bf16[96,768]{1,0:T(8,128)(2,1)}), bf16[96,768]{1,0:T(8,128)(2,1)}) %all-reduce.5.cloned.1.call-update) | async-done | bytes 147472
  (181 shorter events, 131.9 us)
Async XLA Ops:
  7.2 120.1 %copy-start = (bf16[768,2304]{1,0:T(8,128)(2,1)S(1)}, bf16[768,2304]{1,0:T(8,128)(2,1)}, u32[]{:S(2)}) copy-start(bf16[768,2304]{1,0:T(8,128)(2,1)} %param.13) | copy-start | bytes 10616836
  8.3 6.9 collective-permute-start
  11.1 4.1 collective-permute-start.1
  15.2 23.2 %copy-start.28 = (f32[768]{0:T(1024)}, f32[768]{0:T(1024)S(1)}, u32[]{:S(2)}) copy-start(f32[768]{0:T(1024)S(1)} %get-tuple-element.44) | copy-start | bytes 9220
  15.2 23.2 %copy-start.30 = (f32[768]{0:T(1024)}, f32[768]{0:T(1024)S(1)}, u32[]{:S(2)}) copy-start(f32[768]{0:T(1024)S(1)} %get-tuple-element.45) | copy-start | bytes 9220
  17.3 13.4 %collective-permute-start.2 = (bf16[1,34,768]{2,1,0:T(8,128)(2,1)}, bf16[1,34,768]{2,1,0:T(8,128)(2,1)}, u32[]{:S(2)}, u32[]{:S(2)}) collective-permute-start(bf16[1,34,768]{2,1,0:T(8,128)(2,1)} %get-tuple-element.68), channel_id=1, source_target_pairs={{0,32},{32,64},{64,96},{96,128},{128,160},{160,192},{192,224},{1,3... | collective-permute-start | bytes 156680 | tf_op jit(solution)/shard_map/ppermute | solution.py:25
  26.1 9.3 %collective-permute-start.3 = (bf16[1,34,768]{2,1,0:T(8,128)(2,1)}, bf16[1,34,768]{2,1,0:T(8,128)(2,1)}, u32[]{:S(2)}, u32[]{:S(2)}) collective-permute-start(bf16[1,34,768]{2,1,0:T(8,128)(2,1)} %get-tuple-element.69), channel_id=1, source_target_pairs={{32,0},{64,32},{96,64},{128,96},{160,128},{192,160},{224,192},{33,... | collective-permute-start | bytes 156680 | tf_op jit(solution)/shard_map/ppermute | solution.py:26
  30.6 6.5 copy-start.32
  61.1 14.9 %all-to-all-start = ((bf16[8,32,1,1,1,768]{5,1,4,3,2,0:T(8,128)(2,1)}), bf16[8,32,1,1,1,768]{5,1,4,3,2,0:T(8,128)(2,1)}, u32[]{:S(2)}, u32[]{:S(2)}) async-start(bf16[8,32,1,1,1,768]{5,1,4,3,2,0:T(8,128)(2,1)} %bitcast.109), calls=%async_computation | async-start | bytes 786432 | tf_op jit(solution)/shard_map/all_to_all | solution.py:50
  75.9 31.7 %all-to-all-start.5 = ((bf16[1,32,1,8,1,768]{5,3,4,2,0,1:T(8,128)(2,1)}), bf16[1,32,1,8,1,768]{5,3,4,2,0,1:T(8,128)(2,1)}, u32[]{:S(2)}, u32[]{:S(2)}) async-start(bf16[1,32,1,8,1,768]{5,3,4,2,0,1:T(8,128)(2,1)} %copy.78), calls=%async_computation.5 | async-start | bytes 786432 | tf_op jit(solution)/shard_map/all_to_all | solution.py:49
  107.6 18.6 %all-to-all-start.1 = ((bf16[1,32,1,8,1,768]{5,3,4,2,0,1:T(8,128)(2,1)}), bf16[1,32,1,8,1,768]{5,3,4,2,0,1:T(8,128)(2,1)}, u32[]{:S(2)}, u32[]{:S(2)}) async-start(bf16[1,32,1,8,1,768]{5,3,4,2,0,1:T(8,128)(2,1)} %copy.65), calls=%async_computation.1 | async-start | bytes 786432 | tf_op jit(solution)/shard_map/all_to_all | solution.py:49
  155.4 23.1 %all-to-all-start.2 = ((bf16[1,1,1,8,32,768]{5,4,2,1,0,3:T(8,128)(2,1)}), bf16[1,1,1,8,32,768]{5,4,2,1,0,3:T(8,128)(2,1)}, u32[]{:S(2)}, u32[]{:S(2)}) async-start(bf16[1,1,1,8,32,768]{5,4,2,1,0,3:T(8,128)(2,1)} %bitcast.111), calls=%async_computation.2 | async-start | bytes 786432 | tf_op jit(solution)/shard_map/all_to_all | solution.py:61
  178.5 21.4 %all-to-all-start.6 = ((bf16[1,1,1,8,32,768]{5,4,2,1,0,3:T(8,128)(2,1)}), bf16[1,1,1,8,32,768]{5,4,2,1,0,3:T(8,128)(2,1)}, u32[]{:S(2)}, u32[]{:S(2)}) async-start(bf16[1,1,1,8,32,768]{5,4,2,1,0,3:T(8,128)(2,1)} %bitcast.112), calls=%async_computation.6 | async-start | bytes 786432 | tf_op jit(solution)/shard_map/all_to_all | solution.py:61
  199.9 23.2 %all-to-all-start.3 = ((bf16[8,1,1,1,32,768]{5,0,3,2,1,4:T(8,128)(2,1)}), bf16[8,1,1,1,32,768]{5,0,3,2,1,4:T(8,128)(2,1)}, u32[]{:S(2)}, u32[]{:S(2)}) async-start(bf16[8,1,1,1,32,768]{5,0,3,2,1,4:T(8,128)(2,1)} %copy.75), calls=%async_computation.3 | async-start | bytes 786432 | tf_op jit(solution)/shard_map/all_to_all | solution.py:60
  223.1 18.1 %all-to-all-start.7 = ((bf16[8,1,1,1,32,768]{5,0,3,2,1,4:T(8,128)(2,1)}), bf16[8,1,1,1,32,768]{5,0,3,2,1,4:T(8,128)(2,1)}, u32[]{:S(2)}, u32[]{:S(2)}) async-start(bf16[8,1,1,1,32,768]{5,0,3,2,1,4:T(8,128)(2,1)} %copy.88), calls=%async_computation.7 | async-start | bytes 786432 | tf_op jit(solution)/shard_map/all_to_all | solution.py:60
  227.5 233.7 %reduce-scatter.3.cloned.1.call-start = ((), (), s32[]{:S(2)}) async-start(), calls=%async_computation.9 | async-start | bytes 1327104 | tf_op jit(solution)/shard_map/reduce_scatter | solution.py:134
  230.2 495.2 %all-reduce.5.cloned.1.call-start = ((), (), s32[]{:S(2)}) async-start(), calls=%async_computation.10 | async-start | bytes 294912
  255.9 205.3 %copy-start.29 = (f32[768]{0:T(1024)S(1)}, f32[768]{0:T(1024)}, u32[]{:S(2)}) copy-start(f32[768]{0:T(1024)} %copy-done.28) | copy-start | bytes 9220
  255.9 205.3 %copy-start.31 = (f32[768]{0:T(1024)S(1)}, f32[768]{0:T(1024)}, u32[]{:S(2)}) copy-start(f32[768]{0:T(1024)} %copy-done.30) | copy-start | bytes 9220
  255.9 205.3 %copy-start.33 = (f32[768]{0:T(1024)S(1)}, f32[768]{0:T(1024)}, u32[]{:S(2)}) copy-start(f32[768]{0:T(1024)} %get-tuple-element.46) | copy-start | bytes 9220
  266.9 176.8 %collective-permute-start.4 = (bf16[8,1,768]{2,1,0:T(2,128)(2,1)}, bf16[8,1,768]{2,1,0:T(2,128)(2,1)}, u32[]{:S(2)}, u32[]{:S(2)}) collective-permute-start(bf16[8,1,768]{2,1,0:T(2,128)(2,1)} %get-tuple-element.70), channel_id=1, source_target_pairs={{0,1},{1,2},{2,3},{3,4},{4,5},{5,6},{6,7},{7,8},{8,9},{9,10},{10,1... | collective-permute-start | bytes 36872 | tf_op jit(solution)/shard_map/ppermute | solution.py:25
  266.9 176.8 %collective-permute-start.5 = (bf16[8,1,768]{2,1,0:T(2,128)(2,1)}, bf16[8,1,768]{2,1,0:T(2,128)(2,1)}, u32[]{:S(2)}, u32[]{:S(2)}) collective-permute-start(bf16[8,1,768]{2,1,0:T(2,128)(2,1)} %get-tuple-element.71), channel_id=1, source_target_pairs={{1,0},{2,1},{3,2},{4,3},{5,4},{6,5},{7,6},{8,7},{9,8},{10,9},{11,1... | collective-permute-start | bytes 36872 | tf_op jit(solution)/shard_map/ppermute | solution.py:26
  444.6 7.7 %collective-permute-start.6 = (bf16[1,34,768]{2,1,0:T(8,128)(2,1)S(1)}, bf16[1,34,768]{2,1,0:T(8,128)(2,1)S(1)}, u32[]{:S(2)}, u32[]{:S(2)}) collective-permute-start(bf16[1,34,768]{2,1,0:T(8,128)(2,1)S(1)} %get-tuple-element.64), channel_id=1, source_target_pairs={{0,32},{32,64},{64,96},{96,128},{128,160},{160,192},{192,224},{1,3... | collective-permute-start | bytes 156680 | tf_op jit(solution)/shard_map/ppermute | solution.py:25
  449.7 8.9 %collective-permute-start.7 = (bf16[1,34,768]{2,1,0:T(8,128)(2,1)S(1)}, bf16[1,34,768]{2,1,0:T(8,128)(2,1)S(1)}, u32[]{:S(2)}, u32[]{:S(2)}) collective-permute-start(bf16[1,34,768]{2,1,0:T(8,128)(2,1)S(1)} %get-tuple-element.65), channel_id=1, source_target_pairs={{32,0},{64,32},{96,64},{128,96},{160,128},{192,160},{224,192},{33,... | collective-permute-start | bytes 156680 | tf_op jit(solution)/shard_map/ppermute | solution.py:26
  (35 other events, 96.6 us)
Sparse Core Ops, SparseCore 0:
  232.3 83.5 reduce-scatter.2
  461.4 263.9 all-reduce.4
